TPU v7x, 128 devices: a whole 4x4x4 slice. The times are simulated.
128 devices in a mesh: row: 16 (over y, z), col: 8 (over x, core).
Axes of the slice: x: 4, y: 4, z: 4, core: 2. Of those that a mesh axis runs over, the one named last changes fastest.
Arguments:
- matrix: float32 [18432, 18432], P('row', 'col'), as said below
Outputs:
- updated: float32 [18432, 18432], P('row', 'col')
- reflectors: float32 [18432, 512], P('row')
Inputs may be any that keep to these rules, and one draw needn't show every extreme that they name: matrix is symmetric.
All inputs are finite; a program needn't handle non-finite values.
Results may differ from a plain program's by a relative error of at most 0.00016.
Values sent between devices are 32-bit elements; how exact they have to be, the bound alone decides.
A program may use at most 128 MiB of HBM per device.

v0:
```python
import jax
import jax.numpy as jnp
from jax import lax
from jax.sharding import PartitionSpec as P

BAND = 256
PANELS = 2


def spread(array, axis, root):
    mine = lax.axis_index(axis) == root
    return lax.psum(jnp.where(mine, array, jnp.zeros_like(array)), axis)


def contract_first(left, right):
    return lax.dot_general(left, right, (((0,), (0,)), ((), ())), precision=lax.Precision.HIGHEST)


def body(matrix):
    high = lax.Precision.HIGHEST
    current = matrix
    row_count = matrix.shape[0]
    col_count = matrix.shape[1]
    row_start = lax.axis_index("row") * row_count
    col_start = lax.axis_index("col") * col_count
    row_places = row_start + jnp.arange(row_count, dtype=jnp.int32)
    col_places = col_start + jnp.arange(col_count, dtype=jnp.int32)
    columns = jnp.arange(BAND, dtype=jnp.int32)
    identity = jnp.eye(BAND, dtype=jnp.float32)
    stored = []
    history = []
    for which_panel in range(PANELS):
        start = (which_panel + 1) * BAND
        low_edge = which_panel * BAND
        high_edge = (which_panel + 1) * BAND
        local_panel = current[:, low_edge:high_edge]
        panel_rows = spread(local_panel, "col", 0)
        row_strip = spread(current[low_edge:high_edge, :], "row", 0)
        panel_rows = jnp.where(row_places[:, None] >= start, panel_rows, 0.0)
        unit_rows = (row_places[:, None] - start == columns[None, :]).astype(jnp.float32)
        gram_sum, top_block = lax.psum(
            (contract_first(panel_rows, panel_rows), contract_first(unit_rows, panel_rows)), "row"
        )
        factor_low = jnp.linalg.cholesky(gram_sum)
        rows_vec_t = (
            jax.scipy.linalg.solve_triangular(factor_low, panel_rows.T, lower=True) + unit_rows.T
        )
        q_top = jax.scipy.linalg.solve_triangular(factor_low, top_block.T, lower=True).T
        shifted = identity + q_top
        factor_two = jnp.linalg.cholesky(jnp.dot(shifted, shifted.T, precision=high))
        inner = jax.scipy.linalg.solve_triangular(factor_two, identity, lower=True)
        transform = jnp.dot(shifted.T, jnp.dot(inner.T, inner, precision=high), precision=high)
        row_strip = jnp.where(col_places[None, :] >= start, row_strip, 0.0)
        unit_cols = (columns[:, None] == col_places[None, :] - start).astype(jnp.float32)
        cols_vec_t = (
            jax.scipy.linalg.solve_triangular(factor_low, row_strip, lower=True) + unit_cols
        )
        stored.append(rows_vec_t)
        image_part = jnp.dot(rows_vec_t, current, precision=high)
        image_cols = lax.psum(image_part, "row")
        curvature = lax.psum(jnp.dot(image_cols, cols_vec_t.T, precision=high), "col")
        row_part = lax.dot_general(cols_vec_t, current, (((1,), (1,)), ((), ())), precision=high)
        image_rows = lax.psum(row_part, "col")
        middle = jnp.dot(jnp.dot(transform, curvature, precision=high), transform.T, precision=high)
        w_cols = jnp.dot(transform, image_cols, precision=high) - 0.5 * jnp.dot(
            middle.T, cols_vec_t, precision=high
        )
        w_rows = jnp.dot(transform, image_rows, precision=high) - 0.5 * jnp.dot(
            middle.T, rows_vec_t, precision=high
        )
        current = current - contract_first(rows_vec_t, w_cols) - contract_first(w_rows, cols_vec_t)
        history.append((rows_vec_t, w_rows, w_cols, cols_vec_t))
    return (current, jnp.concatenate(stored, axis=0).T)


def solution(mesh):
    placed = (P("row", "col"),)
    return jax.shard_map(
        body,
        mesh=mesh,
        in_specs=placed,
        out_specs=(P("row", "col"), P("row", None)),
        check_vma=False,
    )
```

profile of v0, /device:TPU:0, one launch (start us, length us, event | category | flops | bytes accessed | tf_op | source)
XLA Modules:
  0.0 1102.8 jit_solution(8772189510013273424)
XLA Ops:
  7.2 2.4 slice_select_fusion.3
  9.7 3.2 slice_select_fusion.1
  12.9 63.4 %all-reduce.14.cloned.1.call-done = f32[1152,256]{1,0:T(8,128)} async-done(((f32[1152,256]{1,0:T(8,128)}), f32[1152,256]{1,0:T(8,128)}) %all-reduce.14.cloned.1.call-update) | async-done | bytes 1179664 | tf_op jit(solution)/shard_map/psum | solution.py:12
  76.3 4.9 fusion.14
  82.1 2.1 fusion.8
  84.2 81.0 %all-reduce.16.cloned.1.call-done = f32[256,256]{0,1:T(8,128)} async-done(((f32[256,256]{0,1:T(8,128)}), f32[256,256]{0,1:T(8,128)}) %all-reduce.16.cloned.1.call-update) | async-done | bytes 262160 | tf_op jit(solution)/shard_map/psum | solution.py:41
  167.3 11.7 %cholesky.214 = f32[128,128]{1,0:T(8,128)S(1)} custom-call(f32[128,128]{1,0:T(8,128)S(1)} %cholesky.346), custom_call_target="Cholesky" | custom-call | tf_op jit(solution)/shard_map/jit(cholesky)/cholesky | solution.py:44
  179.0 9.8 custom-call.25
  189.4 11.7 %cholesky.231 = f32[128,128]{1,0:T(8,128)S(1)} custom-call(f32[128,128]{1,0:T(8,128)S(1)} %convolution_subtract_fusion.15), custom_call_target="Cholesky" | custom-call | tf_op jit(solution)/shard_map/jit(cholesky)/cholesky | solution.py:44
  203.2 4.1 while.16
  207.9 19.7 %custom-call.26 = f32[2,128,128]{1,2,0:T(8,128)S(1)} custom-call(f32[2,128,128]{2,1,0:T(8,128)S(1)} %get-tuple-element.60), custom_call_target="InvertDiagBlocksLowerTriangular" | custom-call | tf_op jit(solution)/shard_map/jit(_solve_triangular)/triangular_solve | solution.py:46
  230.3 13.3 %fusion.123 = f32[256,2304]{1,0:T(8,128)} fusion(f32[256,1152]{1,0:T(8,128)S(1)} %maximum_add_fusion.2, f32[1152,2304]{1,0:T(8,128)} %param.8), kind=kOutput, calls=%fused_computation.219 | convolution fusion | flops 8153726976 | bytes 14155776 | tf_op jit(solution)/shard_map/dot_general | solution.py:59
  245.0 109.0 %all-reduce.24.cloned.1.call-done = (f32[256,256]{1,0:T(8,128)}, f32[256,2304]{1,0:T(8,128)}, f32[256,2304]{1,0:T(8,128)}) async-done(((f32[256,256]{1,0:T(8,128)}, f32[256,2304]{1,0:T(8,128)}, f32[256,2304]{1,0:T(8,128)}), (f32[256,256]{1,0:T(8,128)}, f32[256,2304]{1,0:T(8,128)}, f32[256,2304]{1,0:T(8,128)})) %all-reduce.24.cloned.1.call-update) | async-done | bytes 4980752 | tf_op jit(solution)/shard_map/psum | solution.py:41
  354.0 1.8 broadcast_select_fusion.1
  359.4 14.0 %fusion.47 = f32[256,1152]{1,0:T(8,128)} fusion(f32[1152,2304]{1,0:T(8,128)} %param.8, f32[128,2304]{1,0:T(8,128)S(1)} %fusion.81, f32[128,2304]{1,0:T(8,128)S(1)} %fusion.6, s32[2304]{0:T(1024)S(1)} %fusion.95), kind=kOutput, calls=%fused_computation.106 | convolution fusion | flops 8156086272 | bytes 14164992 | tf_op jit(solution)/shard_map/dot_general | solution.py:62
  373.4 3.1 fusion.48
  382.1 1.8 copy.5
  386.2 13.2 %cholesky.248 = f32[128,128]{1,0:T(8,128)} custom-call(f32[128,128]{1,0:T(8,128)} %cholesky.349), custom_call_target="Cholesky" | custom-call | tf_op jit(solution)/shard_map/jit(cholesky)/cholesky | solution.py:50
  399.4 2.0 select_reduce_fusion.5
  403.0 11.3 %custom-call.28 = f32[1,128,128]{1,2,0:T(8,128)} custom-call(f32[1,128,128]{2,1,0:T(8,128)} %get-tuple-element.131), custom_call_target="InvertDiagBlocksLowerTriangular" | custom-call | tf_op jit(solution)/shard_map/jit(cholesky)/cholesky | solution.py:50
  414.3 1.7 constant_dynamic-update-slice_fusion.4
  416.0 1.7 convolution_subtract_fusion.14
  417.7 13.3 %cholesky.265 = f32[128,128]{1,0:T(8,128)} custom-call(f32[128,128]{1,0:T(8,128)} %convolution_subtract_fusion.14), custom_call_target="Cholesky" | custom-call | tf_op jit(solution)/shard_map/jit(cholesky)/cholesky | solution.py:50
  435.9 1.7 select_select_fusion.2
  438.2 8.3 while.17
  439.5 2.9 bitcast_dynamic-update-slice_fusion.9
  443.7 2.9 bitcast_dynamic-update-slice_fusion.9
  446.6 21.1 %custom-call.29 = f32[2,128,128]{1,2,0:T(8,128)} custom-call(f32[2,128,128]{2,1,0:T(8,128)} %get-tuple-element.62), custom_call_target="InvertDiagBlocksLowerTriangular" | custom-call | tf_op jit(solution)/shard_map/jit(_solve_triangular)/triangular_solve | solution.py:51
  469.6 2.0 convolution_subtract_fusion.10
  472.9 1.6 fusion.31
  476.6 5.2 fusion.124
  481.7 53.3 %all-reduce.28.cloned.1.call-done = (f32[256,256]{1,0:T(8,128)}, f32[256,1152]{1,0:T(8,128)}) async-done(((f32[256,256]{1,0:T(8,128)}, f32[256,1152]{1,0:T(8,128)}), (f32[256,256]{1,0:T(8,128)}, f32[256,1152]{1,0:T(8,128)})) %all-reduce.28.cloned.1.call-update) | async-done | bytes 1441808 | tf_op jit(solution)/shard_map/psum | solution.py:61
  535.0 2.6 fusion.127
  540.2 2.6 fusion.1
  542.8 12.7 %convolution_subtract_fusion.3 = f32[1152,2304]{1,0:T(8,128)S(1)} fusion(f32[1152,2304]{1,0:T(8,128)} %param.8, f32[256,1152]{1,0:T(8,128)S(1)} %maximum_add_fusion.2, f32[256,2304]{1,0:T(8,128)S(1)} %fusion.1), kind=kOutput, calls=%fused_computation.11 | convolution fusion | flops 8156381184 | bytes 24772608 | tf_op jit(solution)/shard_map/dot_general | solution.py:16
  555.4 10.0 convolution_subtract_fusion.2
  565.4 4.1 copy-done
  570.7 3.2 slice_select_fusion
  574.0 59.2 %all-reduce.18.cloned.1.call-done = f32[1152,256]{1,0:T(8,128)} async-done(((f32[1152,256]{1,0:T(8,128)}), f32[1152,256]{1,0:T(8,128)}) %all-reduce.18.cloned.1.call-update) | async-done | bytes 1179664 | tf_op jit(solution)/shard_map/psum | solution.py:12
  633.2 4.9 fusion.11
  638.8 2.2 fusion.9
  641.0 81.1 %all-reduce.20.cloned.1.call-done = f32[256,256]{0,1:T(8,128)} async-done(((f32[256,256]{0,1:T(8,128)}), f32[256,256]{0,1:T(8,128)}) %all-reduce.20.cloned.1.call-update) | async-done | bytes 262160 | tf_op jit(solution)/shard_map/psum | solution.py:41
  724.2 11.7 %cholesky.282 = f32[128,128]{1,0:T(8,128)S(1)} custom-call(f32[128,128]{1,0:T(8,128)S(1)} %cholesky.352), custom_call_target="Cholesky" | custom-call | tf_op jit(solution)/shard_map/jit(cholesky)/cholesky | solution.py:44
  735.9 9.8 custom-call.31
  746.2 11.7 %cholesky.299 = f32[128,128]{1,0:T(8,128)S(1)} custom-call(f32[128,128]{1,0:T(8,128)S(1)} %convolution_subtract_fusion.13), custom_call_target="Cholesky" | custom-call | tf_op jit(solution)/shard_map/jit(cholesky)/cholesky | solution.py:44
  760.7 4.5 while.18
  765.2 19.7 %custom-call.32 = f32[2,128,128]{1,2,0:T(8,128)S(1)} custom-call(f32[2,128,128]{2,1,0:T(8,128)S(1)} %get-tuple-element.64), custom_call_target="InvertDiagBlocksLowerTriangular" | custom-call | tf_op jit(solution)/shard_map/jit(_solve_triangular)/triangular_solve | solution.py:46
  787.6 13.7 %fusion.128 = f32[256,2304]{1,0:T(8,128)} fusion(f32[256,1152]{1,0:T(8,128)S(1)} %maximum_add_fusion.3, f32[1152,2304]{1,0:T(8,128)} %copy-done), kind=kOutput, calls=%fused_computation.224 | convolution fusion | flops 8153726976 | bytes 14155776 | tf_op jit(solution)/shard_map/dot_general | solution.py:59
  803.0 3.0 copy.9
  806.0 105.8 %all-reduce.22.cloned.1.call-done = (f32[256,256]{1,0:T(8,128)}, f32[256,2304]{1,0:T(8,128)}, f32[256,2304]{1,0:T(8,128)}) async-done(((f32[256,256]{1,0:T(8,128)}, f32[256,2304]{1,0:T(8,128)}, f32[256,2304]{1,0:T(8,128)}), (f32[256,256]{1,0:T(8,128)}, f32[256,2304]{1,0:T(8,128)}, f32[256,2304]{1,0:T(8,128)})) %all-reduce.22.cloned.1.call-update) | async-done | bytes 4980752 | tf_op jit(solution)/shard_map/psum | solution.py:41
  911.8 1.9 broadcast_select_fusion
  917.2 13.8 %fusion.45 = f32[256,1152]{1,0:T(8,128)} fusion(f32[1152,2304]{1,0:T(8,128)} %copy-done, f32[128,2304]{1,0:T(8,128)S(1)} %fusion.84, f32[128,2304]{1,0:T(8,128)S(1)} %fusion.4, s32[2304]{0:T(1024)S(1)} %fusion.93), kind=kOutput, calls=%fused_computation.104 | convolution fusion | flops 8156086272 | bytes 14164992 | tf_op jit(solution)/shard_map/dot_general | solution.py:62
  931.1 3.1 fusion.46
  936.5 11.7 %cholesky.316 = f32[128,128]{1,0:T(8,128)S(1)} custom-call(f32[128,128]{1,0:T(8,128)S(1)} %cholesky.355), custom_call_target="Cholesky" | custom-call | tf_op jit(solution)/shard_map/jit(cholesky)/cholesky | solution.py:50
  948.3 9.8 custom-call.34
  960.3 11.9 %cholesky.333 = f32[128,128]{1,0:T(8,128)S(1)} custom-call(f32[128,128]{1,0:T(8,128)S(1)} %convolution_subtract_fusion.12), custom_call_target="Cholesky" | custom-call | tf_op jit(solution)/shard_map/jit(cholesky)/cholesky | solution.py:50
  975.0 4.1 while.19
  979.1 19.7 %custom-call.35 = f32[2,128,128]{1,2,0:T(8,128)S(1)} custom-call(f32[2,128,128]{2,1,0:T(8,128)S(1)} %get-tuple-element.66), custom_call_target="InvertDiagBlocksLowerTriangular" | custom-call | tf_op jit(solution)/shard_map/jit(_solve_triangular)/triangular_solve | solution.py:51
  1000.8 5.2 fusion.129
  1006.0 56.9 %all-reduce.26.cloned.1.call-done = (f32[256,256]{1,0:T(8,128)}, f32[256,1152]{1,0:T(8,128)}) async-done(((f32[256,256]{1,0:T(8,128)}, f32[256,1152]{1,0:T(8,128)}), (f32[256,256]{1,0:T(8,128)}, f32[256,1152]{1,0:T(8,128)})) %all-reduce.26.cloned.1.call-update) | async-done | bytes 1441808 | tf_op jit(solution)/shard_map/psum | solution.py:61
  1062.9 2.6 fusion.132
  1068.4 2.5 fusion
  1070.9 12.6 %convolution_subtract_fusion.1 = f32[1152,2304]{1,0:T(8,128)S(1)} fusion(f32[1152,2304]{1,0:T(8,128)} %copy-done, f32[256,1152]{1,0:T(8,128)S(1)} %copy-done.2, f32[256,2304]{1,0:T(8,128)S(1)} %fusion), kind=kOutput, calls=%fused_computation.9 | convolution fusion | flops 8156381184 | bytes 24772608 | tf_op jit(solution)/shard_map/dot_general | solution.py:16
  1083.5 12.2 %convolution_subtract_fusion = f32[1152,2304]{1,0:T(8,128)} fusion(f32[1152,2304]{1,0:T(8,128)S(1)} %convolution_subtract_fusion.1, f32[256,1152]{1,0:T(8,128)S(1)} %fusion.2, f32[128,2304]{1,0:T(8,128)S(1)} %fusion.84, f32[128,2304]{1,0:T(8,128)S(1)} %fusion.4, s32[2304]{0:T(1024)S(1)} %fusion.93), kind=kOutput, calls=%fused_computation.8 | convolution fusion | flops 8158740480 | bytes 24781824 | tf_op jit(solution)/shard_map/dot_general | solution.py:16
  (190 shorter events, 72.9 us)
Async XLA Ops:
  7.2 69.2 %all-reduce.14.cloned.1.call-start = ((), (), s32[]{:S(2)}) async-start(), calls=%async_computation | async-start | bytes 2359296 | tf_op jit(solution)/shard_map/psum | solution.py:12
  9.6 155.6 %all-reduce.16.cloned.1.call-start = ((), (), s32[]{:S(2)}) async-start(), calls=%async_computation.1 | async-start | bytes 524288 | tf_op jit(solution)/shard_map/psum | solution.py:41
  76.3 5.5 copy-start.3
  81.3 272.7 %all-reduce.24.cloned.1.call-start = ((), (), s32[]{:S(2)}) async-start(), calls=%async_computation.5 | async-start | bytes 9961472 | tf_op jit(solution)/shard_map/psum | solution.py:41
  207.3 0.5 copy-start.28
  207.9 149.1 %copy-start.11 = (f32[256,256]{1,0:T(8,128)}, f32[256,256]{1,0:T(8,128)S(1)}, u32[]{:S(2)}) copy-start(f32[256,256]{1,0:T(8,128)S(1)} %get-tuple-element.366) | copy-start | bytes 786436
  227.6 128.3 %copy-start.16 = (f32[2,128,128]{1,2,0:T(8,128)}, f32[2,128,128]{1,2,0:T(8,128)S(1)}, u32[]{:S(2)}) copy-start(f32[2,128,128]{1,2,0:T(8,128)S(1)} %custom-call.26) | copy-start | bytes 393220
  243.6 291.5 %all-reduce.28.cloned.1.call-start = ((), (), s32[]{:S(2)}) async-start(), calls=%async_computation.7 | async-start | bytes 2883584 | tf_op jit(solution)/shard_map/psum | solution.py:61
  357.0 1.2 copy-start.17
  359.3 14.0 %copy-start.5 = (f32[256,2304]{1,0:T(8,128)S(1)}, f32[256,2304]{1,0:T(8,128)}, u32[]{:S(2)}) copy-start(f32[256,2304]{1,0:T(8,128)} %get-tuple-element.106) | copy-start | bytes 7077892
  377.7 2.4 copy-start.15
  380.1 0.7 copy-start.21
  384.9 0.7 copy-start.22
  468.9 0.7 copy-start.20
  471.6 161.6 %all-reduce.18.cloned.1.call-start = ((), (), s32[]{:S(2)}) async-start(), calls=%async_computation.2 | async-start | bytes 2359296 | tf_op jit(solution)/shard_map/psum | solution.py:12
  475.9 0.7 copy-start.9
  535.0 2.7 copy-start.10
  535.0 2.7 copy-start.24
  538.5 1.7 copy-start.7
  565.4 4.1 copy-start
  570.7 151.4 %all-reduce.20.cloned.1.call-start = ((), (), s32[]{:S(2)}) async-start(), calls=%async_computation.3 | async-start | bytes 524288 | tf_op jit(solution)/shard_map/psum | solution.py:41
  633.2 5.2 copy-start.4
  638.1 0.7 copy-start.27
  638.1 273.7 %all-reduce.22.cloned.1.call-start = ((), (), s32[]{:S(2)}) async-start(), calls=%async_computation.4 | async-start | bytes 9961472 | tf_op jit(solution)/shard_map/psum | solution.py:41
  723.1 37.6 %copy-start.29 = (s32[2,2]{1,0:T(2,128)S(1)}, s32[2,2]{1,0:T(2,128)}, u32[]{:S(2)}) copy-start(s32[2,2]{1,0:T(2,128)} %get-tuple-element.391) | copy-start | bytes 52
  765.2 21.5 %copy-start.12 = (f32[256,256]{1,0:T(8,128)}, f32[256,256]{1,0:T(8,128)S(1)}, u32[]{:S(2)}) copy-start(f32[256,256]{1,0:T(8,128)S(1)} %get-tuple-element.367) | copy-start | bytes 786436
  784.9 1.9 copy-start.18
  787.6 13.9 %copy-start.1 = (f32[256,1152]{1,0:T(8,128)}, f32[256,1152]{1,0:T(8,128)S(1)}, u32[]{:S(2)}) copy-start(f32[256,1152]{1,0:T(8,128)S(1)} %maximum_add_fusion.3) | copy-start | bytes 3538948
  801.4 261.5 %all-reduce.26.cloned.1.call-start = ((), (), s32[]{:S(2)}) async-start(), calls=%async_computation.6 | async-start | bytes 2883584 | tf_op jit(solution)/shard_map/psum | solution.py:61
  911.8 1.9 copy-start.19
  913.7 1.2 copy-start.13
  917.2 13.8 %copy-start.6 = (f32[256,2304]{1,0:T(8,128)S(1)}, f32[256,2304]{1,0:T(8,128)}, u32[]{:S(2)}) copy-start(f32[256,2304]{1,0:T(8,128)} %get-tuple-element.103) | copy-start | bytes 7077892
  931.0 3.1 copy-start.26
  935.8 0.7 copy-start.23
  948.3 50.5 %copy-start.14 = (f32[256,256]{0,1:T(8,128)S(1)}, f32[256,256]{0,1:T(8,128)}, u32[]{:S(2)}) copy-start(f32[256,256]{0,1:T(8,128)} %fusion.44) | copy-start | bytes 786436
  1062.9 2.6 copy-start.25
  1065.4 1.3 copy-start.2
  1066.7 1.7 copy-start.8
Sparse Core Ops, SparseCore 0:
  10.9 65.3 all-reduce.13
  81.4 83.7 all-reduce.15
  243.7 110.2 all-reduce.23
  471.7 63.2 all-reduce.27
  570.8 62.3 all-reduce.17
  638.2 83.7 all-reduce.19
  801.5 110.2 all-reduce.21
  999.6 63.1 all-reduce.25
where the time goes:
time: 1110 us; the launch traced here: 1100 us
  waiting for transfers between devices  610 us (55%)
  other arithmetic  249 us (22%)
  matrix products  182 us (16%)
  local copies, waits for them, and re-layouts  39.9 us (4%)
  between operations  20.6 us (2%)
    psum x4, waiting for transfers between devices, body(): lax.psum((contract_first(panel_rows, panel_rows), contract_first(unit_row...  377 us
    psum x2, waiting for transfers between devices, spread(): return lax.psum(jnp.where(mine, array, jnp.zeros_like(array)), axis)  123 us
    psum x2, waiting for transfers between devices, body(): lax.psum(jnp.dot(image_cols, cols_vec_t.T, precision=high), 'col')  110 us
    another operation x14, other arithmetic, body(): jnp.linalg.cholesky(jnp.dot(shifted, shifted.T, precision=high))  78.2 us
    another operation x13, other arithmetic, body(): factor_low = jnp.linalg.cholesky(gram_sum)  68.7 us
    dot_general x8, matrix products, contract_first(): lax.dot_general(left, right, (((0,), (0,)), ((), ())), precision=lax.Prec...  61.5 us
    another operation x4, other arithmetic, body(): inner = jax.scipy.linalg.solve_triangular(factor_two, identity, lower=True)  42.5 us
    another operation x5, other arithmetic, body(): jax.scipy.linalg.solve_triangular(factor_low, panel_rows.T, lower=True)  39.4 us
  transfers between devices with their start and end apart: 8, of which 8 were waited for; matrix products, arithmetic and copies ran while one was open for 3% of the time, Pallas kernels for 0%

commit v1 on v0

--- a/solution.py
+++ b/solution.py
@@ -58,7 +58,9 @@
         stored.append(rows_vec_t)
         image_part = jnp.dot(rows_vec_t, current, precision=high)
         image_cols = lax.psum(image_part, "row")
-        curvature = lax.psum(jnp.dot(image_cols, cols_vec_t.T, precision=high), "col")
+        curvature = jnp.sum(
+            lax.all_gather(jnp.dot(image_cols, cols_vec_t.T, precision=high), "col"), axis=0
+        )
         row_part = lax.dot_general(cols_vec_t, current, (((1,), (1,)), ((), ())), precision=high)
         image_rows = lax.psum(row_part, "col")
         middle = jnp.dot(jnp.dot(transform, curvature, precision=high), transform.T, precision=high)

time: 1110 us -> 1020 us (0.919)
  waiting for transfers between devices: 610 us -> 510 us
    psum x2, waiting for transfers between devices: 110 us -> 0.01 us  [body(): image_rows = lax.psum(row_part, 'col')]
  transfers between devices with their start and end apart: 8 -> 10, of which waited for: 8 -> 7; matrix products, arithmetic and copies ran while one was open for 3% -> 20% of each run, Pallas kernels for 0% -> 0%
where the time goes in v1:
time: 1020 us; the launch traced here: 1010 us
  waiting for transfers between devices  510 us (50%)
  other arithmetic  253 us (25%)
  matrix products  185 us (18%)
  local copies, waits for them, and re-layouts  39.4 us (4%)
  between operations  20.4 us (2%)
    psum x4, waiting for transfers between devices, body(): lax.psum((contract_first(panel_rows, panel_rows), contract_first(unit_row...  377 us
    psum x2, waiting for transfers between devices, spread(): return lax.psum(jnp.where(mine, array, jnp.zeros_like(array)), axis)  123 us
    another operation x14, other arithmetic, body(): jnp.linalg.cholesky(jnp.dot(shifted, shifted.T, precision=high))  78.1 us
    another operation x13, other arithmetic, body(): factor_low = jnp.linalg.cholesky(gram_sum)  68.5 us
    dot_general x8, matrix products, contract_first(): lax.dot_general(left, right, (((0,), (0,)), ((), ())), precision=lax.Prec...  61.5 us
    another operation x4, other arithmetic, body(): inner = jax.scipy.linalg.solve_triangular(factor_two, identity, lower=True)  42.5 us
    another operation x5, other arithmetic, body(): jax.scipy.linalg.solve_triangular(factor_low, panel_rows.T, lower=True)  39.4 us
    dot_general x2, matrix products, body(): lax.dot_general(cols_vec_t, current, (((1,), (1,)), ((), ())), precision=...  27.2 us
  transfers between devices with their start and end apart: 10, of which 7 were waited for; matrix products, arithmetic and copies ran while one was open for 20% of the time, Pallas kernels for 0%

profile of v1, /device:TPU:0, one launch (start us, length us, event | category | flops | bytes accessed | tf_op | source)
XLA Modules:
  0.0 1010.6 jit_solution(17658977333179257208)
XLA Ops:
  7.2 2.4 slice_select_fusion.3
  9.7 3.2 slice_select_fusion.1
  12.9 63.4 %all-reduce.12.cloned.1.call-done = f32[1152,256]{1,0:T(8,128)} async-done(((f32[1152,256]{1,0:T(8,128)}), f32[1152,256]{1,0:T(8,128)}) %all-reduce.12.cloned.1.call-update) | async-done | bytes 1179664 | tf_op jit(solution)/shard_map/psum | solution.py:12
  76.3 4.9 fusion.14
  82.1 2.2 fusion.8
  84.2 81.0 %all-reduce.14.cloned.1.call-done = f32[256,256]{0,1:T(8,128)} async-done(((f32[256,256]{0,1:T(8,128)}), f32[256,256]{0,1:T(8,128)}) %all-reduce.14.cloned.1.call-update) | async-done | bytes 262160 | tf_op jit(solution)/shard_map/psum | solution.py:41
  167.3 11.7 %cholesky.214 = f32[128,128]{1,0:T(8,128)S(1)} custom-call(f32[128,128]{1,0:T(8,128)S(1)} %cholesky.346), custom_call_target="Cholesky" | custom-call | tf_op jit(solution)/shard_map/jit(cholesky)/cholesky | solution.py:44
  179.0 9.8 custom-call.25
  189.3 11.7 %cholesky.231 = f32[128,128]{1,0:T(8,128)S(1)} custom-call(f32[128,128]{1,0:T(8,128)S(1)} %convolution_subtract_fusion.15), custom_call_target="Cholesky" | custom-call | tf_op jit(solution)/shard_map/jit(cholesky)/cholesky | solution.py:44
  203.1 4.1 while.16
  207.9 19.7 %custom-call.26 = f32[2,128,128]{1,2,0:T(8,128)S(1)} custom-call(f32[2,128,128]{2,1,0:T(8,128)S(1)} %get-tuple-element.60), custom_call_target="InvertDiagBlocksLowerTriangular" | custom-call | tf_op jit(solution)/shard_map/jit(_solve_triangular)/triangular_solve | solution.py:46
  230.2 13.3 %fusion.123 = f32[256,2304]{1,0:T(8,128)} fusion(f32[256,1152]{1,0:T(8,128)S(1)} %maximum_add_fusion.2, f32[1152,2304]{1,0:T(8,128)} %param.8), kind=kOutput, calls=%fused_computation.219 | convolution fusion | flops 8153726976 | bytes 14155776 | tf_op jit(solution)/shard_map/dot_general | solution.py:59
  244.9 109.0 %all-reduce.26.cloned.1.call-done = (f32[256,256]{1,0:T(8,128)}, f32[256,2304]{1,0:T(8,128)}, f32[256,2304]{1,0:T(8,128)}) async-done(((f32[256,256]{1,0:T(8,128)}, f32[256,2304]{1,0:T(8,128)}, f32[256,2304]{1,0:T(8,128)}), (f32[256,256]{1,0:T(8,128)}, f32[256,2304]{1,0:T(8,128)}, f32[256,2304]{1,0:T(8,128)})) %all-reduce.26.cloned.1.call-update) | async-done | bytes 4980752 | tf_op jit(solution)/shard_map/psum | solution.py:41
  354.0 1.8 broadcast_select_fusion.1
  359.3 13.7 %fusion.47 = f32[256,1152]{1,0:T(8,128)} fusion(f32[1152,2304]{1,0:T(8,128)} %param.8, f32[128,2304]{1,0:T(8,128)S(1)} %fusion.81, f32[128,2304]{1,0:T(8,128)S(1)} %fusion.6, s32[2304]{0:T(1024)S(1)} %fusion.95), kind=kOutput, calls=%fused_computation.106 | convolution fusion | flops 8156086272 | bytes 14164992 | tf_op jit(solution)/shard_map/dot_general | solution.py:64
  378.7 1.8 copy.5
  380.5 4.7 fusion.48
  388.1 13.2 %cholesky.248 = f32[128,128]{1,0:T(8,128)} custom-call(f32[128,128]{1,0:T(8,128)} %cholesky.349), custom_call_target="Cholesky" | custom-call | tf_op jit(solution)/shard_map/jit(cholesky)/cholesky | solution.py:50
  402.9 2.0 select_reduce_fusion.5
  404.9 11.3 %custom-call.28 = f32[1,128,128]{1,2,0:T(8,128)} custom-call(f32[1,128,128]{2,1,0:T(8,128)} %get-tuple-element.127), custom_call_target="InvertDiagBlocksLowerTriangular" | custom-call | tf_op jit(solution)/shard_map/jit(cholesky)/cholesky | solution.py:50
  416.2 1.7 constant_dynamic-update-slice_fusion.4
  417.9 1.7 convolution_subtract_fusion.14
  419.6 13.2 %cholesky.265 = f32[128,128]{1,0:T(8,128)} custom-call(f32[128,128]{1,0:T(8,128)} %convolution_subtract_fusion.14), custom_call_target="Cholesky" | custom-call | tf_op jit(solution)/shard_map/jit(cholesky)/cholesky | solution.py:50
  437.7 1.7 select_select_fusion.2
  440.1 8.6 while.17
  441.5 2.9 bitcast_dynamic-update-slice_fusion.9
  445.8 2.9 bitcast_dynamic-update-slice_fusion.9
  448.7 21.1 %custom-call.29 = f32[2,128,128]{1,2,0:T(8,128)} custom-call(f32[2,128,128]{2,1,0:T(8,128)} %get-tuple-element.62), custom_call_target="InvertDiagBlocksLowerTriangular" | custom-call | tf_op jit(solution)/shard_map/jit(_solve_triangular)/triangular_solve | solution.py:51
  476.4 3.5 fusion.124
  479.9 3.6 fusion.127
  483.5 2.5 reduce_sum.18
  490.6 2.6 fusion.1
  493.1 12.7 %convolution_subtract_fusion.3 = f32[1152,2304]{1,0:T(8,128)S(1)} fusion(f32[1152,2304]{1,0:T(8,128)} %param.8, f32[256,1152]{1,0:T(8,128)S(1)} %maximum_add_fusion.2, f32[256,2304]{1,0:T(8,128)S(1)} %fusion.1), kind=kOutput, calls=%fused_computation.11 | convolution fusion | flops 8156381184 | bytes 24772608 | tf_op jit(solution)/shard_map/dot_general | solution.py:16
  505.8 10.0 convolution_subtract_fusion.2
  515.8 4.1 copy-done
  521.1 3.2 slice_select_fusion
  524.3 59.3 %all-reduce.18.cloned.1.call-done = f32[1152,256]{1,0:T(8,128)} async-done(((f32[1152,256]{1,0:T(8,128)}), f32[1152,256]{1,0:T(8,128)}) %all-reduce.18.cloned.1.call-update) | async-done | bytes 1179664 | tf_op jit(solution)/shard_map/psum | solution.py:12
  583.7 4.9 fusion.11
  589.3 2.2 fusion.9
  591.4 81.1 %all-reduce.20.cloned.1.call-done = f32[256,256]{0,1:T(8,128)} async-done(((f32[256,256]{0,1:T(8,128)}), f32[256,256]{0,1:T(8,128)}) %all-reduce.20.cloned.1.call-update) | async-done | bytes 262160 | tf_op jit(solution)/shard_map/psum | solution.py:41
  674.6 11.7 %cholesky.282 = f32[128,128]{1,0:T(8,128)S(1)} custom-call(f32[128,128]{1,0:T(8,128)S(1)} %cholesky.352), custom_call_target="Cholesky" | custom-call | tf_op jit(solution)/shard_map/jit(cholesky)/cholesky | solution.py:44
  686.4 9.8 custom-call.31
  696.7 11.7 %cholesky.299 = f32[128,128]{1,0:T(8,128)S(1)} custom-call(f32[128,128]{1,0:T(8,128)S(1)} %convolution_subtract_fusion.13), custom_call_target="Cholesky" | custom-call | tf_op jit(solution)/shard_map/jit(cholesky)/cholesky | solution.py:44
  711.0 4.4 while.18
  715.4 19.7 %custom-call.32 = f32[2,128,128]{1,2,0:T(8,128)S(1)} custom-call(f32[2,128,128]{2,1,0:T(8,128)S(1)} %get-tuple-element.64), custom_call_target="InvertDiagBlocksLowerTriangular" | custom-call | tf_op jit(solution)/shard_map/jit(_solve_triangular)/triangular_solve | solution.py:46
  737.8 13.7 %fusion.128 = f32[256,2304]{1,0:T(8,128)} fusion(f32[256,1152]{1,0:T(8,128)S(1)} %maximum_add_fusion.3, f32[1152,2304]{1,0:T(8,128)} %copy-done), kind=kOutput, calls=%fused_computation.224 | convolution fusion | flops 8153726976 | bytes 14155776 | tf_op jit(solution)/shard_map/dot_general | solution.py:59
  753.2 3.0 copy.9
  756.3 105.8 %all-reduce.24.cloned.1.call-done = (f32[256,256]{1,0:T(8,128)}, f32[256,2304]{1,0:T(8,128)}, f32[256,2304]{1,0:T(8,128)}) async-done(((f32[256,256]{1,0:T(8,128)}, f32[256,2304]{1,0:T(8,128)}, f32[256,2304]{1,0:T(8,128)}), (f32[256,256]{1,0:T(8,128)}, f32[256,2304]{1,0:T(8,128)}, f32[256,2304]{1,0:T(8,128)})) %all-reduce.24.cloned.1.call-update) | async-done | bytes 4980752 | tf_op jit(solution)/shard_map/psum | solution.py:41
  862.1 1.9 broadcast_select_fusion
  867.4 13.5 %fusion.45 = f32[256,1152]{1,0:T(8,128)} fusion(f32[1152,2304]{1,0:T(8,128)} %copy-done, f32[128,2304]{1,0:T(8,128)S(1)} %fusion.84, f32[128,2304]{1,0:T(8,128)S(1)} %fusion.4, s32[2304]{0:T(1024)S(1)} %fusion.93), kind=kOutput, calls=%fused_computation.104 | convolution fusion | flops 8156086272 | bytes 14164992 | tf_op jit(solution)/shard_map/dot_general | solution.py:64
  883.5 4.7 fusion.46
  889.0 11.7 %cholesky.316 = f32[128,128]{1,0:T(8,128)S(1)} custom-call(f32[128,128]{1,0:T(8,128)S(1)} %cholesky.355), custom_call_target="Cholesky" | custom-call | tf_op jit(solution)/shard_map/jit(cholesky)/cholesky | solution.py:50
  900.8 9.8 custom-call.34
  912.8 11.9 %cholesky.333 = f32[128,128]{1,0:T(8,128)S(1)} custom-call(f32[128,128]{1,0:T(8,128)S(1)} %convolution_subtract_fusion.12), custom_call_target="Cholesky" | custom-call | tf_op jit(solution)/shard_map/jit(cholesky)/cholesky | solution.py:50
  927.3 3.8 while.19
  931.1 19.7 %custom-call.35 = f32[2,128,128]{1,2,0:T(8,128)S(1)} custom-call(f32[2,128,128]{2,1,0:T(8,128)S(1)} %get-tuple-element.66), custom_call_target="InvertDiagBlocksLowerTriangular" | custom-call | tf_op jit(solution)/shard_map/jit(_solve_triangular)/triangular_solve | solution.py:51
  952.9 3.5 fusion.129
  956.4 3.6 fusion.132
  960.0 10.4 %all-gather.7.cloned.1.call-done = f32[2048,256]{1,0:T(8,128)} async-done(((f32[256,256]{1,0:T(8,128)}), f32[2048,256]{1,0:T(8,128)}) %all-gather.7.cloned.1.call-update) | async-done | bytes 2097168 | tf_op jit(solution)/shard_map/all_gather | solution.py:62
  970.4 1.8 reduce_sum.19
  973.4 2.7 fusion.2
  976.2 2.5 fusion
  978.7 12.6 %convolution_subtract_fusion.1 = f32[1152,2304]{1,0:T(8,128)S(1)} fusion(f32[1152,2304]{1,0:T(8,128)} %copy-done, f32[256,1152]{1,0:T(8,128)S(1)} %copy-done.2, f32[256,2304]{1,0:T(8,128)S(1)} %fusion), kind=kOutput, calls=%fused_computation.9 | convolution fusion | flops 8156381184 | bytes 24772608 | tf_op jit(solution)/shard_map/dot_general | solution.py:16
  991.3 12.2 %convolution_subtract_fusion = f32[1152,2304]{1,0:T(8,128)} fusion(f32[1152,2304]{1,0:T(8,128)S(1)} %convolution_subtract_fusion.1, f32[256,1152]{1,0:T(8,128)S(1)} %fusion.2, f32[128,2304]{1,0:T(8,128)S(1)} %fusion.84, f32[128,2304]{1,0:T(8,128)S(1)} %fusion.4, s32[2304]{0:T(1024)S(1)} %fusion.93), kind=kOutput, calls=%fused_computation.8 | convolution fusion | flops 8158740480 | bytes 24781824 | tf_op jit(solution)/shard_map/dot_general | solution.py:16
  (192 shorter events, 75.7 us)
Async XLA Ops:
  7.2 69.2 %all-reduce.12.cloned.1.call-start = ((), (), s32[]{:S(2)}) async-start(), calls=%async_computation | async-start | bytes 2359296 | tf_op jit(solution)/shard_map/psum | solution.py:12
  9.6 155.6 %all-reduce.14.cloned.1.call-start = ((), (), s32[]{:S(2)}) async-start(), calls=%async_computation.1 | async-start | bytes 524288 | tf_op jit(solution)/shard_map/psum | solution.py:41
  76.3 5.5 copy-start.3
  81.2 272.7 %all-reduce.26.cloned.1.call-start = ((), (), s32[]{:S(2)}) async-start(), calls=%async_computation.9 | async-start | bytes 9961472 | tf_op jit(solution)/shard_map/psum | solution.py:41
  207.3 0.6 copy-start.25
  207.9 149.1 %copy-start.11 = (f32[256,256]{1,0:T(8,128)}, f32[256,256]{1,0:T(8,128)S(1)}, u32[]{:S(2)}) copy-start(f32[256,256]{1,0:T(8,128)S(1)} %get-tuple-element.358) | copy-start | bytes 786436
  227.5 128.3 %copy-start.16 = (f32[2,128,128]{1,2,0:T(8,128)}, f32[2,128,128]{1,2,0:T(8,128)S(1)}, u32[]{:S(2)}) copy-start(f32[2,128,128]{1,2,0:T(8,128)S(1)} %custom-call.26) | copy-start | bytes 393220
  243.5 236.4 %all-reduce.16.cloned.1.call-start = ((), (), s32[]{:S(2)}) async-start(), calls=%async_computation.2 | async-start | bytes 2359296 | tf_op jit(solution)/shard_map/psum | solution.py:65
  357.0 1.2 copy-start.17
  373.0 110.5 %all-gather.5.cloned.1.call-start = ((), (), s32[]{:S(2)}) async-start(), calls=%async_computation.6 | async-start | bytes 2359296 | tf_op jit(solution)/shard_map/all_gather | solution.py:62
  374.3 2.4 copy-start.15
  376.8 0.7 copy-start.20
  385.3 198.4 %all-reduce.18.cloned.1.call-start = ((), (), s32[]{:S(2)}) async-start(), calls=%async_computation.3 | async-start | bytes 2359296 | tf_op jit(solution)/shard_map/psum | solution.py:12
  386.8 0.7 copy-start.21
  469.8 6.6 copy-start.5
  475.7 0.7 copy-start.9
  486.0 2.9 copy-start.10
  488.9 1.7 copy-start.8
  515.8 4.1 copy-start
  521.1 151.4 %all-reduce.20.cloned.1.call-start = ((), (), s32[]{:S(2)}) async-start(), calls=%async_computation.4 | async-start | bytes 524288 | tf_op jit(solution)/shard_map/psum | solution.py:41
  583.7 5.1 copy-start.4
  588.6 0.7 copy-start.24
  588.6 273.5 %all-reduce.24.cloned.1.call-start = ((), (), s32[]{:S(2)}) async-start(), calls=%async_computation.8 | async-start | bytes 9961472 | tf_op jit(solution)/shard_map/psum | solution.py:41
  673.6 37.5 %copy-start.26 = (s32[2,2]{1,0:T(2,128)S(1)}, s32[2,2]{1,0:T(2,128)}, u32[]{:S(2)}) copy-start(s32[2,2]{1,0:T(2,128)} %get-tuple-element.383) | copy-start | bytes 52
  715.4 21.5 %copy-start.12 = (f32[256,256]{1,0:T(8,128)}, f32[256,256]{1,0:T(8,128)S(1)}, u32[]{:S(2)}) copy-start(f32[256,256]{1,0:T(8,128)S(1)} %get-tuple-element.359) | copy-start | bytes 786436
  735.1 1.9 copy-start.18
  737.8 13.8 %copy-start.1 = (f32[256,1152]{1,0:T(8,128)}, f32[256,1152]{1,0:T(8,128)S(1)}, u32[]{:S(2)}) copy-start(f32[256,1152]{1,0:T(8,128)S(1)} %maximum_add_fusion.3) | copy-start | bytes 3538948
  751.6 204.8 %all-reduce.22.cloned.1.call-start = ((), (), s32[]{:S(2)}) async-start(), calls=%async_computation.5 | async-start | bytes 2359296 | tf_op jit(solution)/shard_map/psum | solution.py:65
  862.1 1.9 copy-start.19
  863.9 1.2 copy-start.13
  880.9 0.9 copy-start.23
  881.0 89.5 %all-gather.7.cloned.1.call-start = ((), (), s32[]{:S(2)}) async-start(), calls=%async_computation.7 | async-start | bytes 2359296 | tf_op jit(solution)/shard_map/all_gather | solution.py:62
  888.3 0.7 copy-start.22
  900.8 50.1 %copy-start.14 = (f32[256,256]{0,1:T(8,128)S(1)}, f32[256,256]{0,1:T(8,128)}, u32[]{:S(2)}) copy-start(f32[256,256]{0,1:T(8,128)} %fusion.44) | copy-start | bytes 786436
  950.8 2.0 copy-start.6
  972.2 1.3 copy-start.2
  973.4 2.7 copy-start.7
Sparse Core Ops, SparseCore 0:
  10.9 65.3 all-reduce.11
  81.4 83.7 all-reduce.13
  243.6 110.2 all-reduce.25
  373.1 63.0 all-reduce.15
  437.8 24.5 all-gather.4
  521.2 62.4 all-reduce.17
  588.7 83.7 all-reduce.19
  751.7 110.2 all-reduce.23
  881.1 63.2 all-reduce.21
  945.9 24.4 all-gather.6
